TPU v7x, 256 devices: a whole 4x4x8 slice. The times are simulated.
256 devices in a mesh: front: 64 (over z, x, core), col: 4 (over y).
Axes of the slice: x: 4, y: 4, z: 8, core: 2. Of those that a mesh axis runs over, the one named last changes fastest.
Arguments:
- leaf_load: bfloat16 [65536, 2048], P('front', 'col'), may hold values from -6 to 6
- leaf_inverse: bfloat16 [65536, 1024], P(('front', 'col')), may hold values from -0.1875 to 0.1875
- leaf_coupling: bfloat16 [32768, 1024], P('front'), may hold values from -0.1875 to 0.1875
- leaf_rowmap: int32 [64, 512], P('front'), may hold values from 0 to 511, each once within a row
- load_first: bfloat16 [16384, 2048], P('front', 'col'), may hold values from -6 to 6
- load_second: bfloat16 [8192, 2048], P('front', 'col'), may hold values from -6 to 6
- load_third: bfloat16 [4096, 2048], P('front', 'col'), may hold values from -6 to 6
- inverse_first: bfloat16 [16384, 512], P('front'), may hold values from -0.15625 to 0.15625
- inverse_second: bfloat16 [8192, 512], P('front'), may hold values from -0.15625 to 0.15625
- inverse_third: bfloat16 [4096, 512], P('front'), may hold values from -0.15625 to 0.15625
- coupling_first: bfloat16 [512, 16384], P(None, 'front'), may hold values from -0.25 to 0.25
- coupling_second: bfloat16 [512, 8192], P(None, 'front'), may hold values from -0.25 to 0.25
- rowmap_first: int32 [32, 512], replicated, may hold values from 0 to 511, each once within a row
- rowmap_second: int32 [16, 512], replicated, may hold values from 0 to 511, each once within a row
- surface_coupling: bfloat16 [192, 1024, 1024], P('front'), may hold values from -0.125 to 0.125
- neighbor_tiles: int32 [64, 2], replicated, may hold values from 0 to 63, as said below
Outputs:
- volume_solution: bfloat16 [65536, 2048], P('front', 'col')
- surface_tiles: bfloat16 [65536, 2048], P('front', 'col')
- solution_first: bfloat16 [16384, 2048], P('front', 'col')
- solution_second: bfloat16 [8192, 2048], P('front', 'col')
- solution_third: bfloat16 [4096, 2048], P('front', 'col')
Inputs may be any that keep to these rules, and one draw needn't show every extreme that they name: Each row of leaf_rowmap is a permutation of the 512 separator rows. Each row of rowmap_first is a permutation of the 512 separator rows. Each row of rowmap_second is a permutation of the 512 separator rows. `neighbor_tiles`: row f names two different tiles, neither equal to f, each within 2 of f; counting each front's own tile, every tile receives 1 to 5 contributions, and some tile receives 5.
All inputs are finite; a program needn't handle non-finite values.
Results may differ from a plain program's by a relative error of at most 0.015.
Values may be sent and summed in bfloat16 or wider, within the bound.
No kernel may reach another device: no remote copies, remote signals or barrier semaphores. Data moves between devices by JAX's collectives and lax.ppermute only.
A program may use at most 128 MiB of HBM per device.

v0:
```python
import jax
import jax.numpy as jnp
from jax import lax
from jax.sharding import PartitionSpec as P


def from_partner(x, axis, bit):
    return lax.ppermute(x, axis, [(i, i ^ 1 << bit) for i in range(lax.axis_size(axis))])


def from_behind(value, axis, steps):
    count = lax.axis_size(axis)
    leading, last = (max(0, -steps), min(count, count - steps))
    return lax.ppermute(value, axis, [(source, source + steps) for source in range(leading, last)])


def climb_tree(own_term, bit_count):
    for level_bit in range(bit_count):
        own_term = own_term + from_partner(own_term, "front", level_bit)
    return own_term


def spread(row_block, bit_count):
    position = lax.axis_index("front")
    for level_bit in range(bit_count):
        partner = from_partner(row_block, "front", level_bit)
        is_upper = position >> level_bit & 1 == 1
        row_block = jnp.where(
            is_upper,
            jnp.concatenate([partner, row_block], axis=0),
            jnp.concatenate([row_block, partner], axis=0),
        )
    return row_block


def pull_back(coupling, lifted):
    return lax.dot_general(
        coupling, lifted, (((0,), (0,)), ((), ())), preferred_element_type=jnp.float32
    )


def local(
    leaf_load,
    leaf_inverse,
    leaf_coupling,
    leaf_rowmap,
    load_first,
    load_second,
    load_third,
    inverse_first,
    inverse_second,
    inverse_third,
    coupling_first,
    coupling_second,
    rowmap_first,
    rowmap_second,
    surface_coupling,
    neighbor_tiles,
):
    position = lax.axis_index("front")
    front_count = lax.axis_size("front")
    factor = lax.all_gather(leaf_inverse, "col", axis=0, tiled=True)
    first_solve = jnp.dot(factor, leaf_load, preferred_element_type=jnp.float32).astype(
        jnp.bfloat16
    )
    sep_order = leaf_coupling.shape[0]
    panel_cols = leaf_load.shape[1]
    partial_value = jnp.dot(leaf_coupling, first_solve, preferred_element_type=jnp.float32)[
        leaf_rowmap[0]
    ]
    load_list = (load_first, load_second, load_third)
    inverses = (inverse_first, inverse_second, inverse_third)
    couplings = (coupling_first, coupling_second)
    rowmaps = (rowmap_first, rowmap_second)
    solved = []
    for level_index in range(3):
        row_count = load_list[level_index].shape[0]
        offset = position % 2 ** (level_index + 1) * row_count
        embedded = lax.dynamic_update_slice_in_dim(
            jnp.zeros((sep_order, panel_cols), jnp.float32),
            load_list[level_index].astype(jnp.float32),
            offset,
            0,
        )
        right_side = climb_tree(embedded - partial_value, level_index + 1).astype(jnp.bfloat16)
        solution = jnp.dot(
            inverses[level_index], right_side, preferred_element_type=jnp.float32
        ).astype(jnp.bfloat16)
        solved.append(solution)
        if level_index < 2:
            row_map = lax.dynamic_index_in_dim(
                rowmaps[level_index], position >> level_index + 1, 0, keepdims=False
            )
            partial_value = jnp.dot(
                couplings[level_index], solution, preferred_element_type=jnp.float32
            )[row_map]
    parent_rows = solved[2]
    results = [None, None, parent_rows]
    for level_index in (1, 0):
        full_vector = spread(parent_rows, level_index + 2)
        row_map = lax.dynamic_index_in_dim(
            rowmaps[level_index], position >> level_index + 1, 0, keepdims=False
        )
        lifted = jnp.zeros((sep_order, panel_cols), jnp.bfloat16).at[row_map].set(full_vector)
        pieces = pull_back(couplings[level_index], lifted).astype(jnp.bfloat16)
        full_pull = spread(pieces, level_index + 1)
        parent_rows = (
            solved[level_index].astype(jnp.float32)
            - jnp.dot(inverses[level_index], full_pull, preferred_element_type=jnp.float32)
        ).astype(jnp.bfloat16)
        results[level_index] = parent_rows
    full_vector = spread(parent_rows, 1)
    lifted = jnp.zeros((sep_order, panel_cols), jnp.bfloat16).at[leaf_rowmap[0]].set(full_vector)
    pulled = pull_back(leaf_coupling, lifted).astype(jnp.bfloat16)
    volume = (
        first_solve.astype(jnp.float32)
        - jnp.dot(factor, pulled, preferred_element_type=jnp.float32)
    ).astype(jnp.bfloat16)
    contribution = jnp.einsum(
        "stf,fp->stp", surface_coupling, volume, preferred_element_type=jnp.float32
    ).astype(jnp.bfloat16)
    tile_sums = contribution[0].astype(jnp.float32)
    for source in (-2, -1, 1, 2):
        arrived = from_behind(contribution[1:], "front", -source)
        anchor = jnp.clip(position + source, 0, front_count - 1)
        aimed_tiles = lax.dynamic_index_in_dim(neighbor_tiles, anchor, 0, keepdims=False)
        matches = (aimed_tiles == position)[:, None, None]
        tile_sums = tile_sums + jnp.sum(
            jnp.where(matches, arrived.astype(jnp.float32), 0.0), axis=0
        )
    return (volume, tile_sums.astype(jnp.bfloat16), results[0], results[1], results[2])


def solution(mesh):
    return jax.shard_map(
        local,
        mesh=mesh,
        in_specs=(
            P("front", "col"),
            P(("front", "col"), None),
            P("front", None),
            P("front", None),
            P("front", "col"),
            P("front", "col"),
            P("front", "col"),
            P("front", None),
            P("front", None),
            P("front", None),
            P(None, "front"),
            P(None, "front"),
            P(),
            P(),
            P("front", None, None),
            P(),
        ),
        out_specs=(
            P("front", "col"),
            P("front", "col"),
            P("front", "col"),
            P("front", "col"),
            P("front", "col"),
        ),
        check_vma=False,
    )
```

profile of v0, /device:TPU:129, one launch (start us, length us, event | category | flops | bytes accessed | tf_op | source)
XLA Modules:
  0.0 308.0 jit_solution(17618731491071650589)
XLA Ops:
  9.7 1.8 convert_dynamic-update-slice_fusion
  11.5 33.0 %all-gather.2.cloned.1.call-done = bf16[1024,1024]{1,0:T(8,128)(2,1)} async-done(((bf16[256,1024]{1,0:T(8,128)(2,1)}), bf16[1024,1024]{1,0:T(8,128)(2,1)}) %all-gather.2.cloned.1.call-update) | async-done | bytes 2097168 | tf_op jit(solution)/shard_map/all_gather | solution.py:62
  44.5 2.8 convolution_convert_fusion
  49.5 1.6 gather_fusion
  51.1 1.5 sub.20
  57.4 1.3 convolution_bitcast_fusion
  59.0 1.6 gather_fusion.1
  60.6 1.4 sub.21
  62.2 2.6 collective-permute-done.1
  65.1 1.3 collective-permute-start.2
  68.1 21.6 %collective-permute-done.2 = f32[512,512]{1,0:T(8,128)S(1)} collective-permute-done((f32[512,512]{1,0:T(8,128)S(1)}, f32[512,512]{1,0:T(8,128)S(1)}, u32[]{:S(2)}, u32[]{:S(2)}) %collective-permute-start.2) | collective-permute-done | bytes 1048608 | tf_op jit(solution)/shard_map/ppermute | solution.py:8
  92.5 1.6 gather_fusion.2
  94.1 1.4 sub.22
  96.6 2.3 collective-permute-done.3
  99.1 1.3 collective-permute-start.4
  100.4 23.2 %collective-permute-done.4 = f32[512,512]{1,0:T(8,128)S(1)} collective-permute-done((f32[512,512]{1,0:T(8,128)S(1)}, f32[512,512]{1,0:T(8,128)S(1)}, u32[]{:S(2)}, u32[]{:S(2)}) %collective-permute-start.4) | collective-permute-done | bytes 1048608 | tf_op jit(solution)/shard_map/ppermute | solution.py:8
  123.8 2.8 collective-permute-start.5
  126.6 22.3 %collective-permute-done.5 = f32[512,512]{1,0:T(8,128)S(1)} collective-permute-done((f32[512,512]{1,0:T(8,128)S(1)}, f32[512,512]{1,0:T(8,128)S(1)}, u32[]{:S(2)}, u32[]{:S(2)}) %collective-permute-start.5) | collective-permute-done | bytes 1048608 | tf_op jit(solution)/shard_map/ppermute | solution.py:8
  149.2 2.2 collective-permute-start.6
  152.3 1.3 collective-permute-start.7
  153.5 3.5 %collective-permute-done.7 = bf16[128,512]{1,0:T(8,128)(2,1)S(1)} collective-permute-done((bf16[128,512]{1,0:T(8,128)(2,1)S(1)}, bf16[128,512]{1,0:T(8,128)(2,1)S(1)}, u32[]{:S(2)}, u32[]{:S(2)}) %collective-permute-start.7) | collective-permute-done | bytes 131104 | tf_op jit(solution)/shard_map/ppermute | solution.py:8
  157.1 3.0 collective-permute-start.8
  160.1 5.5 %collective-permute-done.8 = bf16[256,512]{1,0:T(8,128)(2,1)S(1)} collective-permute-done((bf16[256,512]{1,0:T(8,128)(2,1)S(1)}, bf16[256,512]{1,0:T(8,128)(2,1)S(1)}, u32[]{:S(2)}, u32[]{:S(2)}) %collective-permute-start.8) | collective-permute-done | bytes 262176 | tf_op jit(solution)/shard_map/ppermute | solution.py:8
  165.5 2.6 scatter_custom_fusion
  168.4 2.2 collective-permute-start.9
  171.7 1.3 collective-permute-start.10
  172.9 6.3 %collective-permute-done.10 = bf16[256,512]{1,0:T(8,128)(2,1)S(1)} collective-permute-done((bf16[256,512]{1,0:T(8,128)(2,1)S(1)}, bf16[256,512]{1,0:T(8,128)(2,1)S(1)}, u32[]{:S(2)}, u32[]{:S(2)}) %collective-permute-start.10) | collective-permute-done | bytes 262176 | tf_op jit(solution)/shard_map/ppermute | solution.py:8
  179.6 1.3 collective-permute-start.11
  183.2 6.3 %collective-permute-done.12 = bf16[256,512]{1,0:T(8,128)(2,1)S(1)} collective-permute-done((bf16[256,512]{1,0:T(8,128)(2,1)S(1)}, bf16[256,512]{1,0:T(8,128)(2,1)S(1)}, u32[]{:S(2)}, u32[]{:S(2)}) %collective-permute-start.12) | collective-permute-done | bytes 262176 | tf_op jit(solution)/shard_map/ppermute | solution.py:8
  189.5 2.6 scatter_custom_fusion.1
  192.5 1.3 collective-permute-start.13
  197.0 2.8 scatter_custom_fusion.2
  199.8 4.6 %fusion.4 = bf16[1024,512]{1,0:T(8,128)(2,1)} fusion(bf16[1024,512]{1,0:T(8,128)(2,1)} %copy-done.14, bf16[1024,1024]{1,0:T(8,128)(2,1)} %all-gather.2.cloned.1.call-done, bf16[512,512]{1,0:T(8,128)(2,1)S(1)} %scatter_custom_fusion.2, bf16[512,1024]{1,0:T(8,128)(2,1)S(1)} %copy-done), kind=kOutput, calls=%fused_computation.17 | convolution fusion | flops 1612709888 | bytes 5767168 | tf_op jit(solution)/shard_map/dot_general | solution.py:117
  204.5 6.6 %convert_bitcast_fusion = bf16[3,1024,512]{1,2,0:T(8,128)(2,1)S(1)} fusion(bf16[3,1024,1024]{2,1,0:T(8,128)(2,1)} %param.30, bf16[1024,512]{1,0:T(8,128)(2,1)} %fusion.4), kind=kOutput, calls=%fused_computation.10 | convolution fusion | flops 3222798336 | bytes 10485760 | tf_op jit(solution)/shard_map/stf,fp->stp/dot_general | solution.py:119
  211.3 1.4 copy-done.1
  212.7 4.2 %collective-permute-start.18 = (bf16[2,1024,512]{1,2,0:T(8,128)(2,1)S(1)}, bf16[2,1024,512]{1,2,0:T(8,128)(2,1)}, u32[]{:S(2)}, u32[]{:S(2)}) collective-permute-start(bf16[2,1024,512]{1,2,0:T(8,128)(2,1)S(1)} %slice.18), channel_id=1, source_target_pairs={{8,0},{12,4},{16,8},{20,12},{24,16},{28,20},{32,24},{36,28},{40,32... | collective-permute-start | bytes 6291464 | tf_op jit(solution)/shard_map/ppermute | solution.py:14
  216.9 2.6 collective-permute-start.17
  219.5 3.0 collective-permute-start.16
  222.5 1.9 collective-permute-start.15
  224.7 36.8 %collective-permute-done.18 = bf16[2,1024,512]{1,2,0:T(8,128)(2,1)} collective-permute-done((bf16[2,1024,512]{1,2,0:T(8,128)(2,1)S(1)}, bf16[2,1024,512]{1,2,0:T(8,128)(2,1)}, u32[]{:S(2)}, u32[]{:S(2)}) %collective-permute-start.18) | collective-permute-done | bytes 2097184 | tf_op jit(solution)/shard_map/ppermute | solution.py:14
  261.5 2.6 select_reduce_fusion
  264.1 20.4 %collective-permute-done.17 = bf16[2,1024,512]{1,2,0:T(8,128)(2,1)} collective-permute-done((bf16[2,1024,512]{1,2,0:T(8,128)(2,1)S(1)}, bf16[2,1024,512]{1,2,0:T(8,128)(2,1)}, u32[]{:S(2)}, u32[]{:S(2)}) %collective-permute-start.17) | collective-permute-done | bytes 2097184 | tf_op jit(solution)/shard_map/ppermute | solution.py:14
  284.6 2.6 select_reduce_fusion.1
  287.1 2.6 select_reduce_fusion.2
  289.7 5.2 %collective-permute-done.15 = bf16[2,1024,512]{1,2,0:T(8,128)(2,1)} collective-permute-done((bf16[2,1024,512]{1,2,0:T(8,128)(2,1)S(1)}, bf16[2,1024,512]{1,2,0:T(8,128)(2,1)}, u32[]{:S(2)}, u32[]{:S(2)}) %collective-permute-start.15) | collective-permute-done | bytes 2097184 | tf_op jit(solution)/shard_map/ppermute | solution.py:14
  294.9 2.6 select_reduce_fusion.3
  297.4 2.3 fusion.3
  299.8 1.3 copy.32
  (74 shorter events, 25.1 us)
Async XLA Ops:
  7.2 41.2 %copy-start = (bf16[512,1024]{1,0:T(8,128)(2,1)S(1)}, bf16[512,1024]{1,0:T(8,128)(2,1)}, u32[]{:S(2)}) copy-start(bf16[512,1024]{1,0:T(8,128)(2,1)} %param.18) | copy-start | bytes 3145732
  7.2 37.4 %copy-start.13 = (bf16[1024,512]{1,0:T(8,128)(2,1)S(1)}, bf16[1024,512]{1,0:T(8,128)(2,1)}, u32[]{:S(2)}) copy-start(bf16[1024,512]{1,0:T(8,128)(2,1)} %param.16) | copy-start | bytes 3145732
  7.2 37.4 %all-gather.2.cloned.1.call-start = ((), (), s32[]{:S(2)}) async-start(), calls=%async_computation | async-start | bytes 2621440 | tf_op jit(solution)/shard_map/all_gather | solution.py:62
  47.4 1.0 copy-start.14
  51.1 4.3 %copy-start.9 = (bf16[128,512]{1,0:T(8,128)(2,1)S(1)}, bf16[128,512]{1,0:T(8,128)(2,1)}, u32[]{:S(2)}) copy-start(bf16[128,512]{1,0:T(8,128)(2,1)} %param.21) | copy-start | bytes 393220
  52.6 3.5 %collective-permute-start = (f32[512,512]{1,0:T(8,128)S(1)}, f32[512,512]{1,0:T(8,128)S(1)}, u32[]{:S(2)}, u32[]{:S(2)}) collective-permute-start(f32[512,512]{1,0:T(8,128)S(1)} %sub.20), channel_id=1, source_target_pairs={{0,4},{4,0},{8,12},{12,8},{16,20},{20,16},{24,28},{28,24},{32,36},... | collective-permute-start | bytes 3145736 | tf_op jit(solution)/shard_map/ppermute | solution.py:8
  62.1 5.3 %copy-start.10 = (bf16[64,512]{1,0:T(8,128)(2,1)S(1)}, bf16[64,512]{1,0:T(8,128)(2,1)}, u32[]{:S(2)}) copy-start(bf16[64,512]{1,0:T(8,128)(2,1)} %param.22) | copy-start | bytes 196612
  62.1 2.7 collective-permute-start.1
  65.1 24.7 %collective-permute-start.2 = (f32[512,512]{1,0:T(8,128)S(1)}, f32[512,512]{1,0:T(8,128)S(1)}, u32[]{:S(2)}, u32[]{:S(2)}) collective-permute-start(f32[512,512]{1,0:T(8,128)S(1)} %add.117), channel_id=1, source_target_pairs={{0,8},{4,12},{8,0},{12,4},{16,24},{20,28},{24,16},{28,20},{32,40},... | collective-permute-start | bytes 3145736 | tf_op jit(solution)/shard_map/ppermute | solution.py:8
  95.5 3.4 %collective-permute-start.3 = (f32[512,512]{1,0:T(8,128)S(1)}, f32[512,512]{1,0:T(8,128)S(1)}, u32[]{:S(2)}, u32[]{:S(2)}) collective-permute-start(f32[512,512]{1,0:T(8,128)S(1)} %sub.22), channel_id=1, source_target_pairs={{0,4},{4,0},{8,12},{12,8},{16,20},{20,16},{24,28},{28,24},{32,36},... | collective-permute-start | bytes 3145736 | tf_op jit(solution)/shard_map/ppermute | solution.py:8
  99.1 49.8 %copy-start.11 = (bf16[64,512]{1,0:T(8,128)(2,1)S(1)}, bf16[64,512]{1,0:T(8,128)(2,1)}, u32[]{:S(2)}) copy-start(bf16[64,512]{1,0:T(8,128)(2,1)} %param.25) | copy-start | bytes 196612
  99.1 24.4 %collective-permute-start.4 = (f32[512,512]{1,0:T(8,128)S(1)}, f32[512,512]{1,0:T(8,128)S(1)}, u32[]{:S(2)}, u32[]{:S(2)}) collective-permute-start(f32[512,512]{1,0:T(8,128)S(1)} %add.123), channel_id=1, source_target_pairs={{0,8},{4,12},{8,0},{12,4},{16,24},{20,28},{24,16},{28,20},{32,40},... | collective-permute-start | bytes 3145736 | tf_op jit(solution)/shard_map/ppermute | solution.py:8
  123.8 44.4 %copy-start.3 = (bf16[512,128]{1,0:T(8,128)(2,1)S(1)}, bf16[512,128]{1,0:T(8,128)(2,1)}, u32[]{:S(2)}) copy-start(bf16[512,128]{1,0:T(8,128)(2,1)} %param.27) | copy-start | bytes 393220
  123.8 25.1 %collective-permute-start.5 = (f32[512,512]{1,0:T(8,128)S(1)}, f32[512,512]{1,0:T(8,128)S(1)}, u32[]{:S(2)}, u32[]{:S(2)}) collective-permute-start(f32[512,512]{1,0:T(8,128)S(1)} %add.124), channel_id=1, source_target_pairs={{0,16},{4,20},{8,24},{12,28},{16,0},{20,4},{24,8},{28,12},{32,48},... | collective-permute-start | bytes 3145736 | tf_op jit(solution)/shard_map/ppermute | solution.py:8
  149.1 30.4 %copy-start.6 = (bf16[64,512]{1,0:T(8,128)(2,1)}, bf16[64,512]{1,0:T(8,128)(2,1)S(1)}, u32[]{:S(2)}) copy-start(bf16[64,512]{1,0:T(8,128)(2,1)S(1)} %fusion.7) | copy-start | bytes 196612
  149.1 30.1 %copy-start.7 = (bf16[128,512]{1,0:T(8,128)(2,1)S(1)}, bf16[128,512]{1,0:T(8,128)(2,1)}, u32[]{:S(2)}) copy-start(bf16[128,512]{1,0:T(8,128)(2,1)} %param.24) | copy-start | bytes 393220
  149.2 3.1 collective-permute-start.6
  152.3 4.8 %collective-permute-start.7 = (bf16[128,512]{1,0:T(8,128)(2,1)S(1)}, bf16[128,512]{1,0:T(8,128)(2,1)S(1)}, u32[]{:S(2)}, u32[]{:S(2)}) collective-permute-start(bf16[128,512]{1,0:T(8,128)(2,1)S(1)} %maximum_select_fusion.17), channel_id=1, source_target_pairs={{0,8},{4,12},{8,0},{12,4},{16,24},{20,28},{24,16},{28,20},{32,40},... | collective-permute-start | bytes 393224 | tf_op jit(solution)/shard_map/ppermute | solution.py:8
  157.1 8.4 %collective-permute-start.8 = (bf16[256,512]{1,0:T(8,128)(2,1)S(1)}, bf16[256,512]{1,0:T(8,128)(2,1)S(1)}, u32[]{:S(2)}, u32[]{:S(2)}) collective-permute-start(bf16[256,512]{1,0:T(8,128)(2,1)S(1)} %maximum_select_fusion.14), channel_id=1, source_target_pairs={{0,16},{4,20},{8,24},{12,28},{16,0},{20,4},{24,8},{28,12},{32,48},... | collective-permute-start | bytes 786440 | tf_op jit(solution)/shard_map/ppermute | solution.py:8
  168.4 3.1 %collective-permute-start.9 = (bf16[128,512]{1,0:T(8,128)(2,1)S(1)}, bf16[128,512]{1,0:T(8,128)(2,1)S(1)}, u32[]{:S(2)}, u32[]{:S(2)}) collective-permute-start(bf16[128,512]{1,0:T(8,128)(2,1)S(1)} %fusion.6), channel_id=1, source_target_pairs={{0,4},{4,0},{8,12},{12,8},{16,20},{20,16},{24,28},{28,24},{32,36},... | collective-permute-start | bytes 393224 | tf_op jit(solution)/shard_map/ppermute | solution.py:8
  171.7 20.5 %copy-start.2 = (bf16[512,256]{1,0:T(8,128)(2,1)S(1)}, bf16[512,256]{1,0:T(8,128)(2,1)}, u32[]{:S(2)}) copy-start(bf16[512,256]{1,0:T(8,128)(2,1)} %param.26) | copy-start | bytes 786436
  171.7 23.3 %copy-start.4 = (bf16[256,512]{1,0:T(8,128)(2,1)S(1)}, bf16[256,512]{1,0:T(8,128)(2,1)}, u32[]{:S(2)}) copy-start(bf16[256,512]{1,0:T(8,128)(2,1)} %param.23) | copy-start | bytes 786436
  171.7 7.6 %collective-permute-start.10 = (bf16[256,512]{1,0:T(8,128)(2,1)S(1)}, bf16[256,512]{1,0:T(8,128)(2,1)S(1)}, u32[]{:S(2)}, u32[]{:S(2)}) collective-permute-start(bf16[256,512]{1,0:T(8,128)(2,1)S(1)} %maximum_select_fusion.15), channel_id=1, source_target_pairs={{0,8},{4,12},{8,0},{12,4},{16,24},{20,28},{24,16},{28,20},{32,40},... | collective-permute-start | bytes 786440 | tf_op jit(solution)/shard_map/ppermute | solution.py:8
  179.6 15.8 %copy-start.8 = (bf16[128,512]{1,0:T(8,128)(2,1)}, bf16[128,512]{1,0:T(8,128)(2,1)S(1)}, u32[]{:S(2)}) copy-start(bf16[128,512]{1,0:T(8,128)(2,1)S(1)} %fusion.48) | copy-start | bytes 393220
  179.6 2.3 collective-permute-start.11
  182.0 7.6 %collective-permute-start.12 = (bf16[256,512]{1,0:T(8,128)(2,1)S(1)}, bf16[256,512]{1,0:T(8,128)(2,1)S(1)}, u32[]{:S(2)}, u32[]{:S(2)}) collective-permute-start(bf16[256,512]{1,0:T(8,128)(2,1)S(1)} %maximum_select_fusion.16), channel_id=1, source_target_pairs={{0,8},{4,12},{8,0},{12,4},{16,24},{20,28},{24,16},{28,20},{32,40},... | collective-permute-start | bytes 786440 | tf_op jit(solution)/shard_map/ppermute | solution.py:8
  192.5 2.5 collective-permute-start.13
  195.4 9.1 %copy-start.5 = (bf16[256,512]{1,0:T(8,128)(2,1)}, bf16[256,512]{1,0:T(8,128)(2,1)S(1)}, u32[]{:S(2)}) copy-start(bf16[256,512]{1,0:T(8,128)(2,1)S(1)} %fusion.44) | copy-start | bytes 786436
  195.4 1.6 collective-permute-start.14
  211.1 1.6 copy-start.1
  211.1 13.4 %copy-start.12 = (s32[64,2]{0,1:T(2,128)S(1)}, s32[64,2]{0,1:T(2,128)}, u32[]{:S(2)}) copy-start(s32[64,2]{0,1:T(2,128)} %param.31) | copy-start | bytes 1540
  212.7 48.8 %collective-permute-start.18 = (bf16[2,1024,512]{1,2,0:T(8,128)(2,1)S(1)}, bf16[2,1024,512]{1,2,0:T(8,128)(2,1)}, u32[]{:S(2)}, u32[]{:S(2)}) collective-permute-start(bf16[2,1024,512]{1,2,0:T(8,128)(2,1)S(1)} %slice.18), channel_id=1, source_target_pairs={{8,0},{12,4},{16,8},{20,12},{24,16},{28,20},{32,24},{36,28},{40,32... | collective-permute-start | bytes 6291464 | tf_op jit(solution)/shard_map/ppermute | solution.py:14
  216.9 67.6 %collective-permute-start.17 = (bf16[2,1024,512]{1,2,0:T(8,128)(2,1)S(1)}, bf16[2,1024,512]{1,2,0:T(8,128)(2,1)}, u32[]{:S(2)}, u32[]{:S(2)}) collective-permute-start(bf16[2,1024,512]{1,2,0:T(8,128)(2,1)S(1)} %slice.18), channel_id=1, source_target_pairs={{4,0},{8,4},{12,8},{16,12},{20,16},{24,20},{28,24},{32,28},{36,32}... | collective-permute-start | bytes 6291464 | tf_op jit(solution)/shard_map/ppermute | solution.py:14
  219.5 67.6 %collective-permute-start.16 = (bf16[2,1024,512]{1,2,0:T(8,128)(2,1)S(1)}, bf16[2,1024,512]{1,2,0:T(8,128)(2,1)}, u32[]{:S(2)}, u32[]{:S(2)}) collective-permute-start(bf16[2,1024,512]{1,2,0:T(8,128)(2,1)S(1)} %slice.18), channel_id=1, source_target_pairs={{0,4},{4,8},{8,12},{12,16},{16,20},{20,24},{24,28},{28,32},{32,36}... | collective-permute-start | bytes 6291464 | tf_op jit(solution)/shard_map/ppermute | solution.py:14
  222.5 72.3 %collective-permute-start.15 = (bf16[2,1024,512]{1,2,0:T(8,128)(2,1)S(1)}, bf16[2,1024,512]{1,2,0:T(8,128)(2,1)}, u32[]{:S(2)}, u32[]{:S(2)}) collective-permute-start(bf16[2,1024,512]{1,2,0:T(8,128)(2,1)S(1)} %slice.18), channel_id=1, source_target_pairs={{0,8},{4,12},{8,16},{12,20},{16,24},{20,28},{24,32},{28,36},{32,40... | collective-permute-start | bytes 6291464 | tf_op jit(solution)/shard_map/ppermute | solution.py:14
Sparse Core Ops, SparseCore 0:
  9.8 34.6 all-gather.1
where the time goes:
time: 309 us; the launch traced here: 308 us
  waiting for transfers between devices  195 us (63%)
  starting transfers between devices  33.4 us (11%)
  other arithmetic  30.7 us (10%)
  matrix products  21.3 us (7%)
  between operations  14.5 us (5%)
  local copies, waits for them, and re-layouts  13.1 us (4%)
    ppermute x15, waiting for transfers between devices, from_partner(): lax.ppermute(x, axis, [(i, i ^ 1 << bit) for i in range(lax.axis_size(axi...  98.8 us
    ppermute x4, waiting for transfers between devices, from_behind(): lax.ppermute(value, axis, [(source, source + steps) for source in range(l...  62.4 us
    all_gather x1, waiting for transfers between devices, local(): factor = lax.all_gather(leaf_inverse, 'col', axis=0, tiled=True)  33 us
    ppermute x15, starting transfers between devices, from_partner(): lax.ppermute(x, axis, [(i, i ^ 1 << bit) for i in range(lax.axis_size(axi...  21.7 us
    ppermute x4, starting transfers between devices, from_behind(): lax.ppermute(value, axis, [(source, source + steps) for source in range(l...  11.7 us
    reduce_sum x4, other arithmetic, local(): jnp.sum(jnp.where(matches, arrived.astype(jnp.float32), 0.0), axis=0)  10.3 us
    dot_general x1, matrix products, local(): jnp.einsum('stf,fp->stp', surface_coupling, volume, preferred_element_typ...  6.59 us
  transfers between devices with their start and end apart: 20, of which 18 were waited for; matrix products, arithmetic and copies ran while one was open for 5% of the time, Pallas kernels for 0%

commit v1 on v0

--- a/solution.py
+++ b/solution.py
@@ -59,7 +59,8 @@
 ):
     position = lax.axis_index("front")
     front_count = lax.axis_size("front")
-    factor = lax.all_gather(leaf_inverse, "col", axis=0, tiled=True)
+    sent = jnp.stack([leaf_inverse] * lax.axis_size("col"))
+    factor = jnp.concatenate(lax.all_to_all(sent, "col", 0, 0), axis=0)
     first_solve = jnp.dot(factor, leaf_load, preferred_element_type=jnp.float32).astype(
         jnp.bfloat16
     )

time: 309 us -> 296 us (0.958)
  between operations: 14.5 us -> 1.08 us
  waiting for transfers between devices: 195 us -> 184 us
  starting transfers between devices: 33.4 us -> 38.4 us
  local copies, waits for them, and re-layouts: 13.1 us -> 17.8 us
    all_gather x1 -> x0, waiting for transfers between devices: 33 us -> none  [local(): factor = lax.all_gather(leaf_inverse, 'col', axis=0, tiled=True)]
    all_to_all x0 -> x1, waiting for transfers between devices: none -> 23.5 us  [local(): factor = jnp.concatenate(lax.all_to_all(sent, 'col', 0, 0), axis=0)]
    all_to_all x0 -> x1, starting transfers between devices: none -> 4.31 us  [local(): factor = jnp.concatenate(lax.all_to_all(sent, 'col', 0, 0), axis=0)]
where the time goes in v1:
time: 296 us; the launch traced here: 295 us
  waiting for transfers between devices  184 us (62%)
  starting transfers between devices  38.4 us (13%)
  other arithmetic  30 us (10%)
  matrix products  23.2 us (8%)
  local copies, waits for them, and re-layouts  17.8 us (6%)
    ppermute x15, waiting for transfers between devices, from_partner(): lax.ppermute(x, axis, [(i, i ^ 1 << bit) for i in range(lax.axis_size(axi...  98.6 us
    ppermute x4, waiting for transfers between devices, from_behind(): lax.ppermute(value, axis, [(source, source + steps) for source in range(l...  62.4 us
    all_to_all x1, waiting for transfers between devices, local(): factor = jnp.concatenate(lax.all_to_all(sent, 'col', 0, 0), axis=0)  23.5 us
    ppermute x15, starting transfers between devices, from_partner(): lax.ppermute(x, axis, [(i, i ^ 1 << bit) for i in range(lax.axis_size(axi...  22.7 us
    ppermute x4, starting transfers between devices, from_behind(): lax.ppermute(value, axis, [(source, source + steps) for source in range(l...  11.4 us
    reduce_sum x4, other arithmetic, local(): jnp.sum(jnp.where(matches, arrived.astype(jnp.float32), 0.0), axis=0)  10.3 us
    dot_general x1, matrix products, local(): jnp.einsum('stf,fp->stp', surface_coupling, volume, preferred_element_typ...  6.6 us
  transfers between devices with their start and end apart: 20, of which 18 were waited for; matrix products, arithmetic and copies ran while one was open for 5% of the time, Pallas kernels for 0%

profile of v1, /device:TPU:129, one launch (start us, length us, event | category | flops | bytes accessed | tf_op | source)
XLA Modules:
  0.0 295.0 jit_solution(8618200572228767438)
XLA Ops:
  0.6 2.7 stack.2
  3.4 4.3 %all-to-all-start = ((bf16[4,256,1024]{2,1,0:T(8,128)(2,1)}), bf16[4,256,1024]{2,1,0:T(8,128)(2,1)S(1)}, u32[]{:S(2)}, u32[]{:S(2)}) async-start(bf16[4,256,1024]{2,1,0:T(8,128)(2,1)} %stack.2), calls=%async_computation | async-start | bytes 4194304 | tf_op jit(solution)/shard_map/all_to_all | solution.py:63
  9.7 23.5 %all-to-all-done = bf16[4,256,1024]{2,1,0:T(8,128)(2,1)S(1)} async-done(((bf16[4,256,1024]{2,1,0:T(8,128)(2,1)}), bf16[4,256,1024]{2,1,0:T(8,128)(2,1)S(1)}, u32[]{:S(2)}, u32[]{:S(2)}) %all-to-all-start) | async-done | bytes 2097184 | tf_op jit(solution)/shard_map/all_to_all | solution.py:63
  33.2 3.2 %convolution_convert_fusion = bf16[1024,512]{1,0:T(8,128)(2,1)S(1)} fusion(bf16[1024,1024]{1,0:T(8,128)(2,1)S(1)} %bitcast.68, bf16[1024,512]{1,0:T(8,128)(2,1)} %param.16), kind=kOutput, calls=%fused_computation.18 | convolution fusion | flops 1074266112 | bytes 4194304 | tf_op jit(solution)/shard_map/dot_general | solution.py:64
  37.4 1.8 convolution_bitcast_fusion.2
  39.1 1.6 copy.27
  40.7 1.6 gather_fusion
  42.3 1.5 sub.20
  43.8 1.9 collective-permute-start
  49.6 1.3 convolution_bitcast_fusion
  51.2 1.6 gather_fusion.1
  52.9 1.4 sub.21
  54.5 2.6 collective-permute-done.1
  60.3 21.6 %collective-permute-done.2 = f32[512,512]{1,0:T(8,128)S(1)} collective-permute-done((f32[512,512]{1,0:T(8,128)S(1)}, f32[512,512]{1,0:T(8,128)S(1)}, u32[]{:S(2)}, u32[]{:S(2)}) %collective-permute-start.2) | collective-permute-done | bytes 1048608 | tf_op jit(solution)/shard_map/ppermute | solution.py:8
  84.7 1.6 gather_fusion.2
  86.3 1.4 sub.22
  88.8 2.3 collective-permute-done.3
  92.6 23.1 %collective-permute-done.4 = f32[512,512]{1,0:T(8,128)S(1)} collective-permute-done((f32[512,512]{1,0:T(8,128)S(1)}, f32[512,512]{1,0:T(8,128)S(1)}, u32[]{:S(2)}, u32[]{:S(2)}) %collective-permute-start.4) | collective-permute-done | bytes 1048608 | tf_op jit(solution)/shard_map/ppermute | solution.py:8
  116.0 2.8 collective-permute-start.5
  118.8 22.2 %collective-permute-done.5 = f32[512,512]{1,0:T(8,128)S(1)} collective-permute-done((f32[512,512]{1,0:T(8,128)S(1)}, f32[512,512]{1,0:T(8,128)S(1)}, u32[]{:S(2)}, u32[]{:S(2)}) %collective-permute-start.5) | collective-permute-done | bytes 1048608 | tf_op jit(solution)/shard_map/ppermute | solution.py:8
  141.4 2.2 collective-permute-start.6
  145.8 3.5 %collective-permute-done.7 = bf16[128,512]{1,0:T(8,128)(2,1)S(1)} collective-permute-done((bf16[128,512]{1,0:T(8,128)(2,1)S(1)}, bf16[128,512]{1,0:T(8,128)(2,1)S(1)}, u32[]{:S(2)}, u32[]{:S(2)}) %collective-permute-start.7) | collective-permute-done | bytes 131104 | tf_op jit(solution)/shard_map/ppermute | solution.py:8
  149.3 3.0 %collective-permute-start.8 = (bf16[256,512]{1,0:T(8,128)(2,1)S(1)}, bf16[256,512]{1,0:T(8,128)(2,1)S(1)}, u32[]{:S(2)}, u32[]{:S(2)}) collective-permute-start(bf16[256,512]{1,0:T(8,128)(2,1)S(1)} %maximum_select_fusion.14), channel_id=1, source_target_pairs={{0,16},{4,20},{8,24},{12,28},{16,0},{20,4},{24,8},{28,12},{32,48},... | collective-permute-start | bytes 786440 | tf_op jit(solution)/shard_map/ppermute | solution.py:8
  152.3 5.4 %collective-permute-done.8 = bf16[256,512]{1,0:T(8,128)(2,1)S(1)} collective-permute-done((bf16[256,512]{1,0:T(8,128)(2,1)S(1)}, bf16[256,512]{1,0:T(8,128)(2,1)S(1)}, u32[]{:S(2)}, u32[]{:S(2)}) %collective-permute-start.8) | collective-permute-done | bytes 262176 | tf_op jit(solution)/shard_map/ppermute | solution.py:8
  157.7 2.6 scatter_custom_fusion
  160.7 2.2 collective-permute-start.9
  165.2 6.3 %collective-permute-done.10 = bf16[256,512]{1,0:T(8,128)(2,1)S(1)} collective-permute-done((bf16[256,512]{1,0:T(8,128)(2,1)S(1)}, bf16[256,512]{1,0:T(8,128)(2,1)S(1)}, u32[]{:S(2)}, u32[]{:S(2)}) %collective-permute-start.10) | collective-permute-done | bytes 262176 | tf_op jit(solution)/shard_map/ppermute | solution.py:8
  171.8 1.3 collective-permute-start.11
  175.4 6.3 %collective-permute-done.12 = bf16[256,512]{1,0:T(8,128)(2,1)S(1)} collective-permute-done((bf16[256,512]{1,0:T(8,128)(2,1)S(1)}, bf16[256,512]{1,0:T(8,128)(2,1)S(1)}, u32[]{:S(2)}, u32[]{:S(2)}) %collective-permute-start.12) | collective-permute-done | bytes 262176 | tf_op jit(solution)/shard_map/ppermute | solution.py:8
  181.7 2.6 scatter_custom_fusion.1
  184.7 1.3 collective-permute-start.13
  190.7 3.8 %scatter_custom_fusion.2 = bf16[512,512]{1,0:T(8,128)(2,1)} fusion(s32[512]{0:T(512)S(1)} %bitcast.71, bf16[256,512]{1,0:T(8,128)(2,1)} %copy-done.6, bf16[]{:T(256)} %constant.96, bf16[256,512]{1,0:T(8,128)(2,1)S(1)} %collective-permute-done.14, pred[]{:T(512)S(6)} %eq.65, bf16[]{:T(256)} %constant.70.clone.1), kind=kCustom, calls=%fused_computation.65 | custom fusion | flops 2359296 | bytes 1048581 | tf_op jit(solution)/shard_map/scatter | solution.py:114
  194.5 4.2 %fusion.4 = bf16[1024,512]{1,0:T(8,128)(2,1)} fusion(bf16[1024,512]{1,0:T(8,128)(2,1)} %copy-done.16, bf16[1024,1024]{1,0:T(8,128)(2,1)S(1)} %bitcast.69, bf16[512,512]{1,0:T(8,128)(2,1)} %scatter_custom_fusion.2, bf16[512,1024]{1,0:T(8,128)(2,1)S(1)} %copy-done), kind=kOutput, calls=%fused_computation.17 | convolution fusion | flops 1612709888 | bytes 5767168 | tf_op jit(solution)/shard_map/dot_general | solution.py:118
  198.7 6.6 %convert_bitcast_fusion = bf16[3,1024,512]{1,2,0:T(8,128)(2,1)S(1)} fusion(bf16[3,1024,1024]{2,1,0:T(8,128)(2,1)} %param.30, bf16[1024,512]{1,0:T(8,128)(2,1)} %fusion.4), kind=kOutput, calls=%fused_computation.10 | convolution fusion | flops 3222798336 | bytes 10485760 | tf_op jit(solution)/shard_map/stf,fp->stp/dot_general | solution.py:120
  205.5 1.4 copy-done.1
  206.9 3.9 %collective-permute-start.18 = (bf16[2,1024,512]{1,2,0:T(8,128)(2,1)S(1)}, bf16[2,1024,512]{1,2,0:T(8,128)(2,1)}, u32[]{:S(2)}, u32[]{:S(2)}) collective-permute-start(bf16[2,1024,512]{1,2,0:T(8,128)(2,1)S(1)} %slice.18), channel_id=1, source_target_pairs={{8,0},{12,4},{16,8},{20,12},{24,16},{28,20},{32,24},{36,28},{40,32... | collective-permute-start | bytes 6291464 | tf_op jit(solution)/shard_map/ppermute | solution.py:14
  210.8 2.6 collective-permute-start.17
  213.4 3.0 %collective-permute-start.16 = (bf16[2,1024,512]{1,2,0:T(8,128)(2,1)S(1)}, bf16[2,1024,512]{1,2,0:T(8,128)(2,1)}, u32[]{:S(2)}, u32[]{:S(2)}) collective-permute-start(bf16[2,1024,512]{1,2,0:T(8,128)(2,1)S(1)} %slice.18), channel_id=1, source_target_pairs={{0,4},{4,8},{8,12},{12,16},{16,20},{20,24},{24,28},{28,32},{32,36}... | collective-permute-start | bytes 6291464 | tf_op jit(solution)/shard_map/ppermute | solution.py:14
  216.4 1.9 collective-permute-start.15
  218.6 37.1 %collective-permute-done.18 = bf16[2,1024,512]{1,2,0:T(8,128)(2,1)} collective-permute-done((bf16[2,1024,512]{1,2,0:T(8,128)(2,1)S(1)}, bf16[2,1024,512]{1,2,0:T(8,128)(2,1)}, u32[]{:S(2)}, u32[]{:S(2)}) %collective-permute-start.18) | collective-permute-done | bytes 2097184 | tf_op jit(solution)/shard_map/ppermute | solution.py:14
  255.7 2.6 select_reduce_fusion
  258.3 20.4 %collective-permute-done.17 = bf16[2,1024,512]{1,2,0:T(8,128)(2,1)} collective-permute-done((bf16[2,1024,512]{1,2,0:T(8,128)(2,1)S(1)}, bf16[2,1024,512]{1,2,0:T(8,128)(2,1)}, u32[]{:S(2)}, u32[]{:S(2)}) %collective-permute-start.17) | collective-permute-done | bytes 2097184 | tf_op jit(solution)/shard_map/ppermute | solution.py:14
  278.7 2.6 select_reduce_fusion.1
  281.3 2.6 select_reduce_fusion.2
  283.9 4.8 %collective-permute-done.15 = bf16[2,1024,512]{1,2,0:T(8,128)(2,1)} collective-permute-done((bf16[2,1024,512]{1,2,0:T(8,128)(2,1)S(1)}, bf16[2,1024,512]{1,2,0:T(8,128)(2,1)}, u32[]{:S(2)}, u32[]{:S(2)}) %collective-permute-start.15) | collective-permute-done | bytes 2097184 | tf_op jit(solution)/shard_map/ppermute | solution.py:14
  288.7 2.6 select_reduce_fusion.3
  291.3 2.3 fusion.3
  293.6 1.3 copy.32
  (78 shorter events, 29.3 us)
Async XLA Ops:
  0.6 36.8 %copy-start = (bf16[512,1024]{1,0:T(8,128)(2,1)S(1)}, bf16[512,1024]{1,0:T(8,128)(2,1)}, u32[]{:S(2)}) copy-start(bf16[512,1024]{1,0:T(8,128)(2,1)} %param.18) | copy-start | bytes 3145732
  3.4 4.3 %copy-start.15 = (s32[1,512]{1,0:T(1,128)S(1)}, s32[1,512]{1,0:T(1,128)}, u32[]{:S(2)}) copy-start(s32[1,512]{1,0:T(1,128)} %param.19) | copy-start | bytes 6148
  3.4 5.4 %copy-start.8 = (bf16[256,512]{1,0:T(8,128)(2,1)S(1)}, bf16[256,512]{1,0:T(8,128)(2,1)}, u32[]{:S(2)}) copy-start(bf16[256,512]{1,0:T(8,128)(2,1)} %param.20) | copy-start | bytes 786436
  3.4 29.8 %all-to-all-start = ((bf16[4,256,1024]{2,1,0:T(8,128)(2,1)}), bf16[4,256,1024]{2,1,0:T(8,128)(2,1)S(1)}, u32[]{:S(2)}, u32[]{:S(2)}) async-start(bf16[4,256,1024]{2,1,0:T(8,128)(2,1)} %stack.2), calls=%async_computation | async-start | bytes 4194304 | tf_op jit(solution)/shard_map/all_to_all | solution.py:63
  33.2 3.2 %copy-start.2 = (bf16[4,256,1024]{2,1,0:T(8,128)(2,1)}, bf16[4,256,1024]{2,1,0:T(8,128)(2,1)S(1)}, u32[]{:S(2)}) copy-start(bf16[4,256,1024]{2,1,0:T(8,128)(2,1)S(1)} %all-to-all-done) | copy-start | bytes 6291460
  36.4 1.0 copy-start.16
  42.3 5.2 %copy-start.11 = (bf16[128,512]{1,0:T(8,128)(2,1)S(1)}, bf16[128,512]{1,0:T(8,128)(2,1)}, u32[]{:S(2)}) copy-start(bf16[128,512]{1,0:T(8,128)(2,1)} %param.21) | copy-start | bytes 393220
  43.8 4.5 %collective-permute-start = (f32[512,512]{1,0:T(8,128)S(1)}, f32[512,512]{1,0:T(8,128)S(1)}, u32[]{:S(2)}, u32[]{:S(2)}) collective-permute-start(f32[512,512]{1,0:T(8,128)S(1)} %sub.20), channel_id=1, source_target_pairs={{0,4},{4,0},{8,12},{12,8},{16,20},{20,16},{24,28},{28,24},{32,36},... | collective-permute-start | bytes 3145736 | tf_op jit(solution)/shard_map/ppermute | solution.py:8
  54.3 5.4 %copy-start.12 = (bf16[64,512]{1,0:T(8,128)(2,1)S(1)}, bf16[64,512]{1,0:T(8,128)(2,1)}, u32[]{:S(2)}) copy-start(bf16[64,512]{1,0:T(8,128)(2,1)} %param.22) | copy-start | bytes 196612
  54.3 2.7 collective-permute-start.1
  57.3 24.7 %collective-permute-start.2 = (f32[512,512]{1,0:T(8,128)S(1)}, f32[512,512]{1,0:T(8,128)S(1)}, u32[]{:S(2)}, u32[]{:S(2)}) collective-permute-start(f32[512,512]{1,0:T(8,128)S(1)} %add.117), channel_id=1, source_target_pairs={{0,8},{4,12},{8,0},{12,4},{16,24},{20,28},{24,16},{28,20},{32,40},... | collective-permute-start | bytes 3145736 | tf_op jit(solution)/shard_map/ppermute | solution.py:8
  87.7 3.4 %collective-permute-start.3 = (f32[512,512]{1,0:T(8,128)S(1)}, f32[512,512]{1,0:T(8,128)S(1)}, u32[]{:S(2)}, u32[]{:S(2)}) collective-permute-start(f32[512,512]{1,0:T(8,128)S(1)} %sub.22), channel_id=1, source_target_pairs={{0,4},{4,0},{8,12},{12,8},{16,20},{20,16},{24,28},{28,24},{32,36},... | collective-permute-start | bytes 3145736 | tf_op jit(solution)/shard_map/ppermute | solution.py:8
  91.3 49.8 %copy-start.13 = (bf16[64,512]{1,0:T(8,128)(2,1)S(1)}, bf16[64,512]{1,0:T(8,128)(2,1)}, u32[]{:S(2)}) copy-start(bf16[64,512]{1,0:T(8,128)(2,1)} %param.25) | copy-start | bytes 196612
  91.3 24.4 %collective-permute-start.4 = (f32[512,512]{1,0:T(8,128)S(1)}, f32[512,512]{1,0:T(8,128)S(1)}, u32[]{:S(2)}, u32[]{:S(2)}) collective-permute-start(f32[512,512]{1,0:T(8,128)S(1)} %add.123), channel_id=1, source_target_pairs={{0,8},{4,12},{8,0},{12,4},{16,24},{20,28},{24,16},{28,20},{32,40},... | collective-permute-start | bytes 3145736 | tf_op jit(solution)/shard_map/ppermute | solution.py:8
  116.0 44.4 %copy-start.5 = (bf16[512,128]{1,0:T(8,128)(2,1)S(1)}, bf16[512,128]{1,0:T(8,128)(2,1)}, u32[]{:S(2)}) copy-start(bf16[512,128]{1,0:T(8,128)(2,1)} %param.27) | copy-start | bytes 393220
  116.0 25.1 %collective-permute-start.5 = (f32[512,512]{1,0:T(8,128)S(1)}, f32[512,512]{1,0:T(8,128)S(1)}, u32[]{:S(2)}, u32[]{:S(2)}) collective-permute-start(f32[512,512]{1,0:T(8,128)S(1)} %add.124), channel_id=1, source_target_pairs={{0,16},{4,20},{8,24},{12,28},{16,0},{20,4},{24,8},{28,12},{32,48},... | collective-permute-start | bytes 3145736 | tf_op jit(solution)/shard_map/ppermute | solution.py:8
  141.3 30.4 %copy-start.7 = (bf16[64,512]{1,0:T(8,128)(2,1)}, bf16[64,512]{1,0:T(8,128)(2,1)S(1)}, u32[]{:S(2)}) copy-start(bf16[64,512]{1,0:T(8,128)(2,1)S(1)} %fusion.7) | copy-start | bytes 196612
  141.4 30.1 %copy-start.9 = (bf16[128,512]{1,0:T(8,128)(2,1)S(1)}, bf16[128,512]{1,0:T(8,128)(2,1)}, u32[]{:S(2)}) copy-start(bf16[128,512]{1,0:T(8,128)(2,1)} %param.24) | copy-start | bytes 393220
  141.4 3.1 %collective-permute-start.6 = (bf16[64,512]{1,0:T(8,128)(2,1)S(1)}, bf16[64,512]{1,0:T(8,128)(2,1)S(1)}, u32[]{:S(2)}, u32[]{:S(2)}) collective-permute-start(bf16[64,512]{1,0:T(8,128)(2,1)S(1)} %fusion.7), channel_id=1, source_target_pairs={{0,4},{4,0},{8,12},{12,8},{16,20},{20,16},{24,28},{28,24},{32,36},... | collective-permute-start | bytes 196616 | tf_op jit(solution)/shard_map/ppermute | solution.py:8
  144.5 4.8 %collective-permute-start.7 = (bf16[128,512]{1,0:T(8,128)(2,1)S(1)}, bf16[128,512]{1,0:T(8,128)(2,1)S(1)}, u32[]{:S(2)}, u32[]{:S(2)}) collective-permute-start(bf16[128,512]{1,0:T(8,128)(2,1)S(1)} %maximum_select_fusion.17), channel_id=1, source_target_pairs={{0,8},{4,12},{8,0},{12,4},{16,24},{20,28},{24,16},{28,20},{32,40},... | collective-permute-start | bytes 393224 | tf_op jit(solution)/shard_map/ppermute | solution.py:8
  149.3 8.4 %collective-permute-start.8 = (bf16[256,512]{1,0:T(8,128)(2,1)S(1)}, bf16[256,512]{1,0:T(8,128)(2,1)S(1)}, u32[]{:S(2)}, u32[]{:S(2)}) collective-permute-start(bf16[256,512]{1,0:T(8,128)(2,1)S(1)} %maximum_select_fusion.14), channel_id=1, source_target_pairs={{0,16},{4,20},{8,24},{12,28},{16,0},{20,4},{24,8},{28,12},{32,48},... | collective-permute-start | bytes 786440 | tf_op jit(solution)/shard_map/ppermute | solution.py:8
  160.7 3.1 %collective-permute-start.9 = (bf16[128,512]{1,0:T(8,128)(2,1)S(1)}, bf16[128,512]{1,0:T(8,128)(2,1)S(1)}, u32[]{:S(2)}, u32[]{:S(2)}) collective-permute-start(bf16[128,512]{1,0:T(8,128)(2,1)S(1)} %fusion.6), channel_id=1, source_target_pairs={{0,4},{4,0},{8,12},{12,8},{16,20},{20,16},{24,28},{28,24},{32,36},... | collective-permute-start | bytes 393224 | tf_op jit(solution)/shard_map/ppermute | solution.py:8
  163.9 20.5 %copy-start.4 = (bf16[512,256]{1,0:T(8,128)(2,1)S(1)}, bf16[512,256]{1,0:T(8,128)(2,1)}, u32[]{:S(2)}) copy-start(bf16[512,256]{1,0:T(8,128)(2,1)} %param.26) | copy-start | bytes 786436
  163.9 7.6 %collective-permute-start.10 = (bf16[256,512]{1,0:T(8,128)(2,1)S(1)}, bf16[256,512]{1,0:T(8,128)(2,1)S(1)}, u32[]{:S(2)}, u32[]{:S(2)}) collective-permute-start(bf16[256,512]{1,0:T(8,128)(2,1)S(1)} %maximum_select_fusion.15), channel_id=1, source_target_pairs={{0,8},{4,12},{8,0},{12,4},{16,24},{20,28},{24,16},{28,20},{32,40},... | collective-permute-start | bytes 786440 | tf_op jit(solution)/shard_map/ppermute | solution.py:8
  171.8 3.7 %copy-start.10 = (bf16[128,512]{1,0:T(8,128)(2,1)}, bf16[128,512]{1,0:T(8,128)(2,1)S(1)}, u32[]{:S(2)}) copy-start(bf16[128,512]{1,0:T(8,128)(2,1)S(1)} %fusion.48) | copy-start | bytes 393220
  171.8 2.3 collective-permute-start.11
  174.2 7.6 %collective-permute-start.12 = (bf16[256,512]{1,0:T(8,128)(2,1)S(1)}, bf16[256,512]{1,0:T(8,128)(2,1)S(1)}, u32[]{:S(2)}, u32[]{:S(2)}) collective-permute-start(bf16[256,512]{1,0:T(8,128)(2,1)S(1)} %maximum_select_fusion.16), channel_id=1, source_target_pairs={{0,8},{4,12},{8,0},{12,4},{16,24},{20,28},{24,16},{28,20},{32,40},... | collective-permute-start | bytes 786440 | tf_op jit(solution)/shard_map/ppermute | solution.py:8
  184.7 9.8 %copy-start.3 = (bf16[4,256,1024]{2,1,0:T(8,128)(2,1)S(1)}, bf16[4,256,1024]{2,1,0:T(8,128)(2,1)}, u32[]{:S(2)}) copy-start(bf16[4,256,1024]{2,1,0:T(8,128)(2,1)} %copy-done.2) | copy-start | bytes 6291460
  184.7 2.5 collective-permute-start.13
  188.5 0.7 copy-start.6
  189.2 1.5 collective-permute-start.14
  205.3 1.6 copy-start.1
  205.3 13.1 %copy-start.14 = (s32[64,2]{0,1:T(2,128)S(1)}, s32[64,2]{0,1:T(2,128)}, u32[]{:S(2)}) copy-start(s32[64,2]{0,1:T(2,128)} %param.31) | copy-start | bytes 1540
  206.9 48.8 %collective-permute-start.18 = (bf16[2,1024,512]{1,2,0:T(8,128)(2,1)S(1)}, bf16[2,1024,512]{1,2,0:T(8,128)(2,1)}, u32[]{:S(2)}, u32[]{:S(2)}) collective-permute-start(bf16[2,1024,512]{1,2,0:T(8,128)(2,1)S(1)} %slice.18), channel_id=1, source_target_pairs={{8,0},{12,4},{16,8},{20,12},{24,16},{28,20},{32,24},{36,28},{40,32... | collective-permute-start | bytes 6291464 | tf_op jit(solution)/shard_map/ppermute | solution.py:14
  210.8 67.9 %collective-permute-start.17 = (bf16[2,1024,512]{1,2,0:T(8,128)(2,1)S(1)}, bf16[2,1024,512]{1,2,0:T(8,128)(2,1)}, u32[]{:S(2)}, u32[]{:S(2)}) collective-permute-start(bf16[2,1024,512]{1,2,0:T(8,128)(2,1)S(1)} %slice.18), channel_id=1, source_target_pairs={{4,0},{8,4},{12,8},{16,12},{20,16},{24,20},{28,24},{32,28},{36,32}... | collective-permute-start | bytes 6291464 | tf_op jit(solution)/shard_map/ppermute | solution.py:14
  213.4 67.9 %collective-permute-start.16 = (bf16[2,1024,512]{1,2,0:T(8,128)(2,1)S(1)}, bf16[2,1024,512]{1,2,0:T(8,128)(2,1)}, u32[]{:S(2)}, u32[]{:S(2)}) collective-permute-start(bf16[2,1024,512]{1,2,0:T(8,128)(2,1)S(1)} %slice.18), channel_id=1, source_target_pairs={{0,4},{4,8},{8,12},{12,16},{16,20},{20,24},{24,28},{28,32},{32,36}... | collective-permute-start | bytes 6291464 | tf_op jit(solution)/shard_map/ppermute | solution.py:14
  216.4 72.3 %collective-permute-start.15 = (bf16[2,1024,512]{1,2,0:T(8,128)(2,1)S(1)}, bf16[2,1024,512]{1,2,0:T(8,128)(2,1)}, u32[]{:S(2)}, u32[]{:S(2)}) collective-permute-start(bf16[2,1024,512]{1,2,0:T(8,128)(2,1)S(1)} %slice.18), channel_id=1, source_target_pairs={{0,8},{4,12},{8,16},{12,20},{16,24},{20,28},{24,32},{28,36},{32,40... | collective-permute-start | bytes 6291464 | tf_op jit(solution)/shard_map/ppermute | solution.py:14
